TPU v7x, 32 devices: a whole 2x2x4 slice. The times are simulated.
32 devices in a mesh: group: 2 (over x), replica: 16 (over z, y, core).
Axes of the slice: x: 2, y: 2, z: 4, core: 2. Of those that a mesh axis runs over, the one named last changes fastest.
Arguments:
- block_in: bfloat16 [16, 1024, 1024], P('replica', 'group'), may hold values from -6 to 6
- attn_gain: bfloat16 [1024], P('group'), may hold values from 0.5 to 1.5
- query_weight: bfloat16 [1024, 1024], P('group'), may hold values from -0.25 to 0.25
- key_weight: bfloat16 [1024, 512], P('group'), may hold values from -0.25 to 0.25
- value_weight: bfloat16 [1024, 512], P('group'), may hold values from -0.1875 to 0.1875
- out_weight: bfloat16 [1024, 1024], P('group'), may hold values from -1.5 to 1.5
- ffn_gain: bfloat16 [1024], P('group'), may hold values from 0.5 to 1.5
- router_weight: bfloat16 [1024, 16], P('group'), may hold values from -0.09375 to 0.09375
- expert_in: bfloat16 [16, 1024, 1024], P('group'), may hold values from -0.1875 to 0.1875
- expert_out: bfloat16 [16, 1024, 512], P('group'), may hold values from -1.5 to 1.5
- routes: int32 [16, 1024, 8], P('replica', 'group'), may hold values from 0 to 15, all different within a row; in each aligned block of 512 rows (0 to 511, 512 to 1023, ..., all dimensions but the last counted through in order) at most 384 rows name the same one
- prefix: int32 [16], P('replica'), may hold values from 102 to 512, as said below
- cotangent: bfloat16 [16, 1024, 1024], P('replica', 'group'), may hold values from -6 to 6
Outputs:
- block_out: bfloat16 [16, 1024, 1024], P('replica', 'group')
- input_grad: float32 [16, 1024, 1024], P('replica', 'group')
- attn_gain_grad: float32 [1024], P(('group', 'replica'))
- query_grad: float32 [1024, 1024], P(('group', 'replica'))
- key_grad: float32 [1024, 512], P(('group', 'replica'))
- value_grad: float32 [1024, 512], P(('group', 'replica'))
- out_grad: float32 [1024, 1024], P(None, ('group', 'replica'))
- ffn_gain_grad: float32 [1024], P(('group', 'replica'))
- router_grad: float32 [1024, 16], P(('group', 'replica'))
- expert_in_grad: float32 [16, 1024, 1024], P(None, ('group', 'replica'))
- expert_out_grad: float32 [16, 1024, 512], P(None, ('group', 'replica'))
Inputs may be any that keep to these rules, and one draw needn't show every extreme that they name: `routes`: each token names 8 different experts. Among the 512 tokens of one sequence block no expert is named more than 384 times, and in every draw some expert is named exactly 384 times by some block. Some sequence has a prefix of exactly 512.
All inputs are finite; a program needn't handle non-finite values.
Results may differ from a plain program's by a relative error of at most 0.017.
The roundings to bfloat16 on the way count: a program that leaves them out, or rounds other values in their place, can miss the bound.
Values may be sent and summed in bfloat16 or wider, within the bound.
No kernel may reach another device: no remote copies, remote signals or barrier semaphores. Data moves between devices by JAX's collectives and lax.ppermute only.
A program may use at most 448 MiB of HBM per device.

v0:
```python
import math
import jax
import jax.numpy as jnp
from jax import lax
from jax.sharding import PartitionSpec as P

HEADS = 16
KV_HEADS = 8
HEAD = 64
FF = 512
TOP = 8
EXPERTS = 16
CAP = 384
EPSILON = 1e-06
THETA_BASE = 10000.0
MASKED = -1e30
HIGHEST = lax.Precision.HIGHEST


def from_behind(value, axis, steps):
    count = lax.axis_size(axis)
    first, last = (max(0, -steps), min(count, count - steps))
    return lax.ppermute(value, axis, [(source, source + steps) for source in range(first, last)])


def normalize(values, gain):
    return values * lax.rsqrt(jnp.mean(values * values, -1, keepdims=True) + EPSILON) * gain


def rope_tables(positions, head_size):
    half_head = head_size // 2
    frequency = THETA_BASE ** (-jnp.arange(half_head, dtype=jnp.float32) * 2.0 / head_size)
    angles = positions.astype(jnp.float32)[:, None] * frequency[None, :]
    return (jnp.cos(angles)[:, None, :], jnp.sin(angles)[:, None, :])


def rotate(values, cosine, sine_table):
    half_head = values.shape[-1] // 2
    first_half = values[..., :half_head]
    second_half = values[..., half_head:]
    return jnp.concatenate(
        [
            first_half * cosine - second_half * sine_table,
            second_half * cosine + first_half * sine_table,
        ],
        -1,
    )


def rotate_back(gradient, cosine, sine_table):
    half_head = gradient.shape[-1] // 2
    first_half = gradient[..., :half_head]
    second_half = gradient[..., half_head:]
    return jnp.concatenate(
        [
            first_half * cosine + second_half * sine_table,
            second_half * cosine - first_half * sine_table,
        ],
        -1,
    )


def contract_rows(left, right):
    return lax.dot_general(
        left, right, (((0,), (0,)), ((), ())), preferred_element_type=jnp.float32
    )


def contract_cols(left, right):
    return lax.dot_general(
        left, right, (((1,), (1,)), ((), ())), preferred_element_type=jnp.float32
    )


def expert_forward(rows, weight_in, weight_out):
    gate_up = jnp.einsum("ecd,edf->ecf", rows, weight_in, preferred_element_type=jnp.float32)
    hidden = (jax.nn.silu(gate_up[..., :FF]) * gate_up[..., FF:]).astype(jnp.bfloat16)
    outputs = jnp.einsum("ecf,edf->ecd", hidden, weight_out, preferred_element_type=jnp.float32)
    return (gate_up, hidden, outputs)


def expert_backward(rows, gate_up, hidden, grad_rows, weight_in, weight_out):
    grad_hidden = jnp.einsum(
        "ecd,edf->ecf", grad_rows, weight_out, preferred_element_type=jnp.float32
    )
    grad_out_weight = jnp.einsum(
        "ecd,ecf->edf", grad_rows, hidden, preferred_element_type=jnp.float32
    )
    gate_part = gate_up[..., :FF]
    up_part = gate_up[..., FF:]
    sigmoid = jax.nn.sigmoid(gate_part)
    grad_gate = grad_hidden * up_part * sigmoid * (1.0 + gate_part * (1.0 - sigmoid))
    grad_up = grad_hidden * (gate_part * sigmoid)
    grad_gate_up = jnp.concatenate([grad_gate, grad_up], -1).astype(jnp.bfloat16)
    grad_in_weight = jnp.einsum(
        "ecd,ecf->edf", rows, grad_gate_up, preferred_element_type=jnp.float32
    )
    grad_rows_in = jnp.einsum(
        "ecf,edf->ecd", grad_gate_up, weight_in, preferred_element_type=jnp.float32
    )
    return (grad_rows_in, grad_in_weight, grad_out_weight)


def on_device(
    block_in,
    attn_gain,
    query_weight,
    key_weight,
    value_weight,
    out_weight,
    ffn_gain,
    router_weight,
    expert_in,
    expert_out,
    routes,
    prefix,
    cotangent,
):
    tokens = block_in.shape[1]
    width = block_in.shape[2]
    half_index = lax.axis_index("group")
    inputs = block_in[0].astype(jnp.float32)
    token_routes = routes[0]
    prefix_len = prefix[0]
    grad_out = cotangent[0].astype(jnp.float32)
    groups = HEADS // KV_HEADS
    score_scale = 1.0 / math.sqrt(HEAD)
    rows_block = min(tokens, 512)
    block_count = tokens // rows_block
    positions = half_index * tokens + jnp.arange(tokens, dtype=jnp.int32)
    key_positions = jnp.concatenate([positions - tokens, positions])
    cosine, sine_table = rope_tables(positions, HEAD)
    gain_attn, weight_q, weight_k, weight_v, weight_o = (
        lax.all_gather(attn_gain, "group", axis=0, tiled=True),
        lax.all_gather(query_weight, "group", axis=0, tiled=True),
        lax.all_gather(key_weight, "group", axis=0, tiled=True),
        lax.all_gather(value_weight, "group", axis=0, tiled=True),
        lax.all_gather(out_weight, "group", axis=0, tiled=True),
    )
    normed_attn_f, attn_norm_pull = jax.vjp(normalize, inputs, gain_attn.astype(jnp.float32))
    normed_attn = normed_attn_f.astype(jnp.bfloat16)
    query_pre = jnp.dot(normed_attn, weight_q, preferred_element_type=jnp.float32).reshape(
        tokens, HEADS, HEAD
    )
    key_pre = jnp.dot(normed_attn, weight_k, preferred_element_type=jnp.float32).reshape(
        tokens, KV_HEADS, HEAD
    )
    queries = rotate(query_pre, cosine, sine_table).astype(jnp.bfloat16)
    own_keys = rotate(key_pre, cosine, sine_table).astype(jnp.bfloat16)
    own_values = (
        jnp.dot(normed_attn, weight_v, preferred_element_type=jnp.float32)
        .astype(jnp.bfloat16)
        .reshape(tokens, KV_HEADS, HEAD)
    )
    prev_keys, prev_values = from_behind((own_keys, own_values), "group", 1)
    all_keys = jnp.concatenate([prev_keys, own_keys], 0)
    all_values = jnp.concatenate([prev_values, own_values], 0)
    query_blocks = queries.reshape(block_count, rows_block, KV_HEADS, groups, HEAD)
    position_blocks = positions.reshape(block_count, rows_block)

    def masked_scores(query_block, query_pos):
        scores = (
            jnp.einsum("qkgd,jkd->kgqj", query_block, all_keys, preferred_element_type=jnp.float32)
            * score_scale
        )
        visible = (key_positions[None, :] >= 0) & (
            (key_positions[None, :] <= query_pos[:, None]) | (key_positions[None, :] < prefix_len)
        )
        return jnp.where(visible, scores, MASKED)

    def forward_block(operands):
        query_block, query_pos = operands
        scores = masked_scores(query_block, query_pos)
        row_peak = jnp.max(scores, -1, keepdims=True)
        exponent = jnp.exp(scores - row_peak)
        row_total = jnp.sum(exponent, -1, keepdims=True)
        weights_low = (exponent / row_total).astype(jnp.bfloat16)
        attended_block = jnp.einsum(
            "kgqj,jkd->qkgd", weights_low, all_values, preferred_element_type=jnp.float32
        )
        return (attended_block.astype(jnp.bfloat16), row_peak + jnp.log(row_total))

    attended_blocks, log_totals = lax.map(forward_block, (query_blocks, position_blocks))
    attended = attended_blocks.reshape(tokens, HEADS * HEAD)
    residual = inputs + jnp.dot(attended, weight_o, preferred_element_type=jnp.float32)
    gain_ffn, router_full, expert_in_full, expert_out_full = (
        lax.all_gather(ffn_gain, "group", axis=0, tiled=True),
        lax.all_gather(router_weight, "group", axis=0, tiled=True),
        lax.all_gather(expert_in, "group", axis=0, tiled=True),
        lax.all_gather(expert_out, "group", axis=0, tiled=True),
    )
    normed_ffn_f, ffn_norm_pull = jax.vjp(normalize, residual, gain_ffn.astype(jnp.float32))
    normed_ffn = normed_ffn_f.astype(jnp.bfloat16)
    logits = jnp.dot(normed_ffn, router_full, preferred_element_type=jnp.float32)
    gate_probs = jax.nn.softmax(jnp.take_along_axis(logits, token_routes, 1), -1)
    expert_ids = jnp.arange(EXPERTS, dtype=jnp.int32)
    member = (token_routes[:, :, None] == expert_ids[None, None, :]).astype(jnp.int32)
    per_token = jnp.sum(member, 1)
    before = jnp.cumsum(per_token, 0) - per_token
    slot_index = jnp.sum(member * before[:, None, :], 2)
    flat_slot = (token_routes * CAP + slot_index).reshape(-1)
    token_ids = jnp.repeat(jnp.arange(tokens, dtype=jnp.int32), TOP)
    source = jnp.zeros((EXPERTS * CAP,), jnp.int32).at[flat_slot].set(token_ids)
    filled = jnp.zeros((EXPERTS * CAP,), jnp.bfloat16).at[flat_slot].set(1.0)
    gate_rows = jnp.zeros((EXPERTS * CAP,), jnp.float32).at[flat_slot].set(gate_probs.reshape(-1))
    buffer = (normed_ffn[source] * filled[:, None]).reshape(EXPERTS, CAP, width)
    gate_up, hidden, expert_rows = expert_forward(buffer, expert_in_full, expert_out_full)
    picked = expert_rows.reshape(EXPERTS * CAP, width)[flat_slot].reshape(tokens, TOP, width)
    block_out = (residual + jnp.sum(gate_probs[:, :, None] * picked, 1)).astype(jnp.bfloat16)
    grad_gates = jnp.sum(picked * grad_out[:, None, :], 2)
    grad_expert_rows = (
        (grad_out[source] * gate_rows[:, None]).astype(jnp.bfloat16).reshape(EXPERTS, CAP, width)
    )
    back_in, back_out = (
        lax.all_gather(expert_in, "group", axis=0, tiled=True),
        lax.all_gather(expert_out, "group", axis=0, tiled=True),
    )
    grad_buffer, grad_in_weight, grad_out_weight = expert_backward(
        buffer, gate_up, hidden, grad_expert_rows, back_in, back_out
    )
    expert_in_grad, expert_out_grad = (
        lax.psum_scatter(grad_in_weight, ("group", "replica"), scatter_dimension=1, tiled=True),
        lax.psum_scatter(grad_out_weight, ("group", "replica"), scatter_dimension=1, tiled=True),
    )
    grad_from_experts = jnp.sum(
        grad_buffer.reshape(EXPERTS * CAP, width)[flat_slot].reshape(tokens, TOP, width), 1
    )
    mean_term = jnp.sum(gate_probs * grad_gates, 1, keepdims=True)
    grad_chosen = gate_probs * (grad_gates - mean_term)
    grad_logits = jnp.sum(
        grad_chosen[:, :, None]
        * (token_routes[:, :, None] == expert_ids[None, None, :]).astype(jnp.float32),
        1,
    )
    router_f = router_full.astype(jnp.float32)
    router_full_grad = lax.dot_general(
        normed_ffn.astype(jnp.float32), grad_logits, (((0,), (0,)), ((), ())), precision=HIGHEST
    )
    grad_normed_ffn = grad_from_experts + lax.dot_general(
        grad_logits, router_f, (((1,), (1,)), ((), ())), precision=HIGHEST
    )
    grad_res_norm, ffn_gain_full_grad = ffn_norm_pull(grad_normed_ffn)
    grad_residual = grad_out + grad_res_norm
    grad_res_low = grad_residual.astype(jnp.bfloat16)
    out_full_grad = contract_rows(attended, grad_res_low)
    grad_attended = contract_cols(grad_res_low, weight_o).astype(jnp.bfloat16)
    grad_blocks = grad_attended.reshape(block_count, rows_block, KV_HEADS, groups, HEAD)

    def backward_block(running, operands):
        grad_key_sum, grad_value_sum = running
        query_block, query_pos, grad_block, log_total = operands
        scores = masked_scores(query_block, query_pos)
        probability = jnp.exp(scores - log_total)
        grad_probs = jnp.einsum(
            "qkgd,jkd->kgqj", grad_block, all_values, preferred_element_type=jnp.float32
        )
        row_delta = jnp.sum(probability * grad_probs, -1, keepdims=True)
        grad_scores = (probability * (grad_probs - row_delta)).astype(jnp.bfloat16)
        grad_query = (
            jnp.einsum("kgqj,jkd->qkgd", grad_scores, all_keys, preferred_element_type=jnp.float32)
            * score_scale
        )
        grad_key_sum = (
            grad_key_sum
            + jnp.einsum(
                "kgqj,qkgd->jkd", grad_scores, query_block, preferred_element_type=jnp.float32
            )
            * score_scale
        )
        grad_value_sum = grad_value_sum + jnp.einsum(
            "kgqj,qkgd->jkd",
            probability.astype(jnp.bfloat16),
            grad_block,
            preferred_element_type=jnp.float32,
        )
        return ((grad_key_sum, grad_value_sum), grad_query)

    empty_keys = jnp.zeros((2 * tokens, KV_HEADS, HEAD), jnp.float32)
    (grad_keys_all, grad_values_all), grad_query_blocks = lax.scan(
        backward_block,
        (empty_keys, empty_keys),
        (query_blocks, position_blocks, grad_blocks, log_totals),
    )
    back_keys, back_values = (
        from_behind(grad_keys_all[:tokens].astype(jnp.bfloat16), "group", -1).astype(jnp.float32),
        from_behind(grad_values_all[:tokens].astype(jnp.bfloat16), "group", -1).astype(jnp.float32),
    )
    grad_keys = grad_keys_all[tokens:] + back_keys
    grad_values = grad_values_all[tokens:] + back_values
    grad_query_pre = (
        rotate_back(grad_query_blocks.reshape(tokens, HEADS, HEAD), cosine, sine_table)
        .astype(jnp.bfloat16)
        .reshape(tokens, HEADS * HEAD)
    )
    grad_key_pre = (
        rotate_back(grad_keys, cosine, sine_table)
        .astype(jnp.bfloat16)
        .reshape(tokens, KV_HEADS * HEAD)
    )
    grad_value_pre = grad_values.astype(jnp.bfloat16).reshape(tokens, KV_HEADS * HEAD)
    query_full_grad = contract_rows(normed_attn, grad_query_pre)
    key_full_grad = contract_rows(normed_attn, grad_key_pre)
    value_full_grad = contract_rows(normed_attn, grad_value_pre)
    grad_normed_attn = (
        contract_cols(grad_query_pre, weight_q)
        + contract_cols(grad_key_pre, weight_k)
        + contract_cols(grad_value_pre, weight_v)
    )
    grad_in_norm, attn_gain_full_grad = attn_norm_pull(grad_normed_attn)
    input_grad = grad_residual + grad_in_norm
    attn_gain_grad, query_grad, key_grad, value_grad, out_grad, ffn_gain_grad, router_grad = (
        lax.psum_scatter(
            attn_gain_full_grad, ("group", "replica"), scatter_dimension=0, tiled=True
        ),
        lax.psum_scatter(query_full_grad, ("group", "replica"), scatter_dimension=0, tiled=True),
        lax.psum_scatter(key_full_grad, ("group", "replica"), scatter_dimension=0, tiled=True),
        lax.psum_scatter(value_full_grad, ("group", "replica"), scatter_dimension=0, tiled=True),
        lax.psum_scatter(out_full_grad, ("group", "replica"), scatter_dimension=1, tiled=True),
        lax.psum_scatter(ffn_gain_full_grad, ("group", "replica"), scatter_dimension=0, tiled=True),
        lax.psum_scatter(router_full_grad, ("group", "replica"), scatter_dimension=0, tiled=True),
    )
    return (
        block_out[None],
        input_grad[None],
        attn_gain_grad,
        query_grad,
        key_grad,
        value_grad,
        out_grad,
        ffn_gain_grad,
        router_grad,
        expert_in_grad,
        expert_out_grad,
    )


def solution(mesh):
    placed = (
        P("replica", "group", None),
        P("group"),
        P("group", None),
        P("group", None),
        P("group", None),
        P("group", None),
        P("group"),
        P("group", None),
        P("group", None, None),
        P("group", None, None),
        P("replica", "group", None),
        P("replica"),
        P("replica", "group", None),
    )
    return jax.shard_map(
        on_device,
        mesh=mesh,
        in_specs=placed,
        out_specs=(
            P("replica", "group", None),
            P("replica", "group", None),
            P(("group", "replica")),
            P(("group", "replica"), None),
            P(("group", "replica"), None),
            P(("group", "replica"), None),
            P(None, ("group", "replica")),
            P(("group", "replica")),
            P(("group", "replica"), None),
            P(None, ("group", "replica"), None),
            P(None, ("group", "replica"), None),
        ),
        check_vma=False,
    )
```

profile of v0, /device:TPU:1, one launch (start us, length us, event | category | flops | bytes accessed | tf_op | source)
XLA Modules:
  0.0 2654.7 jit_solution(8985328769214327289)
XLA Ops:
  12.5 3.7 all-gather
  16.2 3.2 all-gather.1
  20.0 3.9 all_gather.35
  26.8 28.6 %scatter_custom_fusion.1 = bf16[6144]{0:T(1024)(128)(2,1)S(1)} fusion(s32[4096]{0:T(1024)S(1)} %bitcast.237, bf16[4096]{0:T(1024)(128)(2,1)S(1)} %broadcast.399, bf16[]{:T(256)} %constant.114.clone.1), kind=kCustom, calls=%fused_computation.149 | custom fusion | bytes 12290 | tf_op jit(solution)/shard_map/scatter | solution.py:204
  57.8 15.5 scatter_custom_fusion
  73.4 1.5 bitcast_convert_fusion
  74.9 27.4 %gather_fusion.2 = f32[6144,1024]{1,0:T(8,128)} fusion(f32[512,1024]{1,0:T(8,128)S(1)} %bitcast_convert_fusion, s32[6144]{0:T(1024)S(1)} %fusion.64), kind=kCustom, calls=%fused_computation.2 | custom fusion | bytes 50356224 | tf_op jit(solution)/shard_map/gather | solution.py:212
  102.2 24.8 copy.88
  127.3 1.6 or_and_fusion
  129.0 2.9 convolution_convert_fusion.1
  131.9 4.3 collective-permute-start
  136.1 1.8 copy.75
  139.9 2.3 collective-permute-start.1
  142.3 4.3 copy.76
  146.6 3.7 fusion.45
  150.8 3.2 collective-permute-done.1
  154.0 17.8 fusion.91
  171.8 14.2 fusion.3
  186.0 13.8 fusion.41
  199.9 3.3 multiply_reduce_fusion.2
  204.8 26.8 %gather_fusion = bf16[6144,1024]{1,0:T(8,128)(2,1)} fusion(bf16[512,1024]{1,0:T(8,128)(2,1)S(1)} %multiply_convert_fusion.6, s32[6144]{0:T(1024)S(1)} %fusion.64), kind=kCustom, calls=%fused_computation | custom fusion | bytes 25190400 | tf_op jit(solution)/shard_map/gather | solution.py:206
  232.4 33.0 %gather_fusion.4 = f32[4096]{0:T(1024)S(1)} fusion(f32[512,16]{0,1:T(8,128)S(1)} %fusion.92, s32[4096]{0:T(1024)S(1)} %copy-done.4), kind=kCustom, calls=%fused_computation.4 | custom fusion | bytes 65536 | tf_op jit(solution)/shard_map/jit(take_along_axis)/gather | solution.py:195
  266.6 16.1 scatter_custom_fusion.2
  282.7 15.5 copy.85
  299.8 218.3 %all-gather.17.cloned.1.call-done = bf16[16,1024,1024]{2,1,0:T(8,128)(2,1)} async-done(((bf16[8,1024,1024]{2,1,0:T(8,128)(2,1)}), bf16[16,1024,1024]{2,1,0:T(8,128)(2,1)}) %all-gather.17.cloned.1.call-update) | async-done | bytes 33554448 | tf_op jit(solution)/shard_map/all_gather | solution.py:189
  518.1 30.7 %fusion.14 = f32[16,384,1024]{2,1,0:T(8,128)} fusion(bf16[16,1024,1024]{2,1,0:T(8,128)(2,1)} %all-gather.17.cloned.1.call-done, bf16[16,384,1024]{1,2,0:T(8,128)(2,1)} %copy.85, bf16[16,384]{1,0:T(8,128)(2,1)S(1)} %copy-done.38), kind=kOutput, calls=%fused_computation.36 | convolution fusion | flops 12891193344 | bytes 71315456 | tf_op jit(solution)/shard_map/ecd,edf->ecf/dot_general | solution.py:76
  548.8 171.8 %all-gather.19.cloned.1.call-done = bf16[16,1024,512]{2,1,0:T(8,128)(2,1)} async-done(((bf16[8,1024,512]{2,1,0:T(8,128)(2,1)}), bf16[16,1024,512]{2,1,0:T(8,128)(2,1)}) %all-gather.19.cloned.1.call-update) | async-done | bytes 16777232 | tf_op jit(solution)/shard_map/all_gather | solution.py:190
  720.6 30.4 %multiply_convert_fusion.2 = (bf16[16,384,512]{2,1,0:T(8,128)(2,1)}, bf16[16,384,512]{2,1,0:T(8,128)(2,1)}, bf16[16,384,512]{2,1,0:T(8,128)(2,1)}) fusion(f32[16,384,1024]{2,1,0:T(8,128)} %fusion.14, bf16[16,1024,512]{2,1,0:T(8,128)(2,1)} %all-gather.19.cloned.1.call-done, f32[16,384,1024]{1,2,0:T(8,128)} %copy.88, f32[16,384]{1,0:T(8,128)S(1)} %mul.437), kind=kOutput, calls=%fused_computation.30 | convolution fusion | flops 6502219776 | bytes 86007808 | tf_op jit(solution)/shard_map/ecd,edf->ecf/dot_general | solution.py:83
  750.9 26.2 fusion.16
  777.2 30.5 %gather_fusion.3 = f32[4096,1024]{1,0:T(8,128)} fusion(f32[6144,1024]{1,0:T(8,128)} %bitcast.198, s32[4096]{0:T(1024)S(1)} %copy-done.44), kind=kCustom, calls=%fused_computation.3 | custom fusion | bytes 33570816 | tf_op jit(solution)/shard_map/gather | solution.py:226
  807.6 9.7 bitcast_reduce_fusion
  817.3 22.7 fusion.93
  840.0 30.6 %gather_fusion.1 = f32[4096,1024]{1,0:T(8,128)} fusion(f32[6144,1024]{1,0:T(8,128)} %bitcast.197, s32[4096]{0:T(1024)S(1)} %copy-done.44), kind=kCustom, calls=%fused_computation.1 | custom fusion | bytes 33570816 | tf_op jit(solution)/shard_map/gather | solution.py:208
  870.6 10.8 fusion.8
  883.6 2.0 fusion.96
  885.6 3.9 multiply_reduce_fusion
  889.6 1.6 fusion.34
  891.2 1.3 copy-done.10
  894.6 13.3 fusion.38
  908.0 1.3 collective-permute-start.3
  909.3 22.9 fusion
  933.6 2.3 fusion.51
  936.0 27.5 %fusion.2 = bf16[8,2,512,1024]{2,3,1,0:T(8,128)(2,1)} fusion(f32[8,1024,512,2]{2,1,3,0:T(8,128)} %get-tuple-element.105, f32[8,2,512,1024]{2,3,1,0:T(8,128)} %get-tuple-element.100, f32[8,2,512]{2,1,0:T(2,128)S(1)} %get-tuple-element.104, f32[8,2,512]{2,1,0:T(2,128)S(1)} %bitcast.222), kind=kLoop, calls=%fused_computation.12 | loop fusion | flops 33554432 | bytes 83951616 | tf_op jit(solution)/shard_map/while/body/eval_jaxpr/convert_element_type | solution.py:258
  963.5 11.3 fusion.37
  974.9 1.3 collective-permute-start.2
  976.2 13.4 collective-permute-done.2
  990.8 2.2 fusion.53
  993.1 4.5 fusion.58
  998.5 9.0 convolution_multiply_fusion
  1008.9 3.4 fusion.49
  1013.1 24.6 fusion.19
  1038.4 33.7 %fusion.12 = f32[16,1024,1024]{2,1,0:T(8,128)} fusion(bf16[16,384,1024]{1,2,0:T(8,128)(2,1)} %copy.85, bf16[16,384,512]{2,1,0:T(8,128)(2,1)} %get-tuple-element.71, bf16[16,384,512]{2,1,0:T(8,128)(2,1)} %get-tuple-element.70, bf16[16,384]{1,0:T(8,128)(2,1)S(1)} %copy-done.39), kind=kOutput, calls=%fused_computation.34 | convolution fusion | flops 12916359168 | bytes 92286976 | tf_op jit(solution)/shard_map/ecd,ecf->edf/dot_general | solution.py:95
  1072.1 4.5 fusion.94
  1076.6 1.4 copy.107
  1078.0 2.3 fusion.95
  1080.5 2.5 fusion.29
  1083.1 40.6 %all-reduce.2 = (f32[1024]{0:T(1024)S(1)}, f32[1024]{0:T(1024)S(1)}) all-reduce(f32[1024]{0:T(1024)S(1)} %get-tuple-element.66, f32[1024]{0:T(1024)S(1)} %copy-done.60), channel_id=2, replica_groups=mesh['group'=2,'replica'=16] {'group','replica'}, use_global_device_ids=true, to_apply=%region_22.23.clone | all-reduce | flops 2048 | bytes 16384
  1124.9 3.5 fusion.36
  1128.3 31.6 %reduce-scatter.14.cloned.1.call-done = f32[32,512]{1,0:T(8,128)} async-done(((f32[1024,512]{1,0:T(8,128)}), f32[32,512]{1,0:T(8,128)}) %reduce-scatter.14.cloned.1.call-update) | async-done | bytes 65552 | tf_op jit(solution)/shard_map/reduce_scatter | solution.py:317
  1159.9 136.1 %reduce-scatter.12.cloned.1.call-done = f32[32,512]{1,0:T(8,128)} async-done(((f32[1024,512]{1,0:T(8,128)}), f32[32,512]{1,0:T(8,128)}) %reduce-scatter.12.cloned.1.call-update) | async-done | bytes 65552 | tf_op jit(solution)/shard_map/reduce_scatter | solution.py:316
  1296.0 139.9 %reduce-scatter.16.cloned.1.call-done = f32[1024,32]{0,1:T(8,128)} async-done(((f32[1024,1024]{0,1:T(8,128)}), f32[1024,32]{0,1:T(8,128)}) %reduce-scatter.16.cloned.1.call-update) | async-done | bytes 131088 | tf_op jit(solution)/shard_map/reduce_scatter | solution.py:318
  1435.9 140.7 %reduce-scatter.10.cloned.1.call-done = f32[32,1024]{1,0:T(8,128)} async-done(((f32[1024,1024]{1,0:T(8,128)}), f32[32,1024]{1,0:T(8,128)}) %reduce-scatter.10.cloned.1.call-update) | async-done | bytes 131088 | tf_op jit(solution)/shard_map/reduce_scatter | solution.py:315
  1576.6 362.2 %reduce-scatter.20.cloned.1.call-done = f32[16,32,512]{2,1,0:T(8,128)} async-done(((f32[16,1024,512]{2,1,0:T(8,128)}), f32[16,32,512]{2,1,0:T(8,128)}) %reduce-scatter.20.cloned.1.call-update) | async-done | bytes 1048592 | tf_op jit(solution)/shard_map/reduce_scatter | solution.py:223
  1938.8 709.0 %reduce-scatter.18.cloned.1.call-done = f32[16,32,1024]{2,1,0:T(8,128)} async-done(((f32[16,1024,1024]{2,1,0:T(8,128)}), f32[16,32,1024]{2,1,0:T(8,128)}) %reduce-scatter.18.cloned.1.call-update) | async-done | bytes 2097168 | tf_op jit(solution)/shard_map/reduce_scatter | solution.py:222
  (231 shorter events, 30.1 us)
Async XLA Ops:
  7.2 121.8 %all-gather.9.cloned.1.call-start = ((), (), s32[]{:S(2)}) async-start(), calls=%async_computation.7 | async-start | bytes 1572864 | tf_op jit(solution)/shard_map/all_gather | solution.py:137
  7.9 128.2 %all-gather.11.cloned.1.call-start = ((), (), s32[]{:S(2)}) async-start(), calls=%async_computation.8 | async-start | bytes 1572864 | tf_op jit(solution)/shard_map/all_gather | solution.py:136
  8.7 133.6 %all-gather.13.cloned.1.call-start = ((), (), s32[]{:S(2)}) async-start(), calls=%async_computation.9 | async-start | bytes 3145728 | tf_op jit(solution)/shard_map/all_gather | solution.py:135
  9.4 190.5 %all-gather.15.cloned.1.call-start = ((), (), s32[]{:S(2)}) async-start(), calls=%async_computation.10 | async-start | bytes 3145728 | tf_op jit(solution)/shard_map/all_gather | solution.py:138
  10.0 508.1 %all-gather.17.cloned.1.call-start = ((), (), s32[]{:S(2)}) async-start(), calls=%async_computation.11 | async-start | bytes 50331648 | tf_op jit(solution)/shard_map/all_gather | solution.py:189
  10.6 1.8 copy-start.61
  10.6 5.6 copy-start.62
  10.6 9.4 copy-start.59
  10.6 710.0 %all-gather.19.cloned.1.call-start = ((), (), s32[]{:S(2)}) async-start(), calls=%async_computation.12 | async-start | bytes 25165824 | tf_op jit(solution)/shard_map/all_gather | solution.py:190
  11.2 1065.4 %reduce-scatter.22.cloned.1.call-start = ((), (), s32[]{:S(2)}) async-start(), calls=%async_computation.19 | async-start | bytes 540672
  11.5 61.9 %copy-start.14 = (s32[1,512,8]{2,1,0:T(8,128)}, s32[1,512,8]{2,1,0:T(8,128)S(1)}, u32[]{:S(2)}) copy-start(s32[1,512,8]{2,1,0:T(8,128)S(1)} %copy.78) | copy-start | bytes 49156
  12.4 13.0 copy-start.55
  12.4 134.2 %copy-start.51 = (f32[512]{0:T(512)}, f32[512]{0:T(512)S(1)}, u32[]{:S(2)}) copy-start(f32[512]{0:T(512)S(1)} %fusion.74) | copy-start | bytes 6148
  16.2 130.4 %copy-start.45 = (f32[2,1,512]{2,1,0:T(1,128)}, f32[2,1,512]{2,1,0:T(1,128)S(1)}, u32[]{:S(2)}) copy-start(f32[2,1,512]{2,1,0:T(1,128)S(1)} %convert_element_type.171) | copy-start | bytes 12292
  26.2 47.2 %copy-start.48 = (s32[4096,1]{0,1:T(1,128)}, s32[4096,1]{0,1:T(1,128)S(1)}, u32[]{:S(2)}) copy-start(s32[4096,1]{0,1:T(1,128)S(1)} %compare_select_fusion.1) | copy-start | bytes 49156
  74.9 27.4 %copy-start = (f32[512,1024]{1,0:T(8,128)}, f32[512,1024]{1,0:T(8,128)S(1)}, u32[]{:S(2)}) copy-start(f32[512,1024]{1,0:T(8,128)S(1)} %bitcast_convert_fusion) | copy-start | bytes 6291460
  127.3 23.1 copy-start.28
  127.3 23.1 copy-start.30
  131.9 54.1 %collective-permute-start = (bf16[512,8,64]{0,2,1:T(8,128)(2,1)}, bf16[512,8,64]{0,2,1:T(8,128)(2,1)}, u32[]{:S(2)}, u32[]{:S(2)}) collective-permute-start(bf16[512,8,64]{0,2,1:T(8,128)(2,1)} %bitcast.2), channel_id=1, source_target_pairs={{0,16},{1,17},{2,18},{3,19},{4,20},{5,21},{6,22},{7,23},{8,24},{9,... | collective-permute-start | bytes 1572872 | tf_op jit(solution)/shard_map/ppermute | solution.py:23
  139.0 15.0 copy-start.21
  139.0 15.0 copy-start.23
  139.9 14.1 collective-permute-start.1
  150.4 3.6 copy-start.37
  150.8 21.0 copy-start.25
  150.8 21.0 copy-start.26
  199.8 3.4 copy-start.13
  199.9 4.7 copy-start.49
  203.2 1.6 copy-start.57
  203.2 1.5 copy-start.53
  204.8 26.8 %copy-start.2 = (bf16[512,1024]{1,0:T(8,128)(2,1)}, bf16[512,1024]{1,0:T(8,128)(2,1)S(1)}, u32[]{:S(2)}) copy-start(bf16[512,1024]{1,0:T(8,128)(2,1)S(1)} %multiply_convert_fusion.6) | copy-start | bytes 3145732
  204.8 26.8 %copy-start.40 = (bf16[1024,16]{0,1:T(8,128)(2,1)S(1)}, bf16[1024,16]{0,1:T(8,128)(2,1)}, u32[]{:S(2)}) copy-start(bf16[1024,16]{0,1:T(8,128)(2,1)} %all_gather.35) | copy-start | bytes 98308
  232.4 33.2 %copy-start.15 = (s32[1,512,8]{2,1,0:T(8,128)S(1)}, s32[1,512,8]{2,1,0:T(8,128)}, u32[]{:S(2)}) copy-start(s32[1,512,8]{2,1,0:T(8,128)} %copy-done.14) | copy-start | bytes 49156
  282.7 437.9 %copy-start.42 = (f32[16,384]{1,0:T(8,128)}, f32[16,384]{1,0:T(8,128)S(1)}, u32[]{:S(2)}) copy-start(f32[16,384]{1,0:T(8,128)S(1)} %mul.437) | copy-start | bytes 73732
  282.7 235.4 %copy-start.38 = (bf16[16,384]{1,0:T(8,128)(2,1)S(1)}, bf16[16,384]{1,0:T(8,128)(2,1)}, u32[]{:S(2)}) copy-start(bf16[16,384]{1,0:T(8,128)(2,1)} %mul.431) | copy-start | bytes 36868
  750.9 26.2 copy-start.44
  807.6 9.7 copy-start.7
  840.0 30.6 %copy-start.1 = (f32[512,1024]{1,0:T(8,128)S(1)}, f32[512,1024]{1,0:T(8,128)}, u32[]{:S(2)}) copy-start(f32[512,1024]{1,0:T(8,128)} %copy-done) | copy-start | bytes 6291460
  840.0 30.6 %copy-start.19 = (f32[512,8]{1,0:T(8,128)S(1)}, f32[512,8]{1,0:T(8,128)}, u32[]{:S(2)}) copy-start(f32[512,8]{1,0:T(8,128)} %fusion.61) | copy-start | bytes 49156
  870.6 12.9 copy-start.36
  881.4 2.2 copy-start.3
  881.4 4.2 copy-start.9
  881.4 4.2 copy-start.41
  881.4 4.2 copy-start.50
  881.4 4.2 copy-start.54
  885.6 3.9 copy-start.58
  885.6 4.0 copy-start.12
  885.6 4.0 copy-start.20
  889.6 3.0 copy-start.27
  894.4 265.4 %reduce-scatter.14.cloned.1.call-start = ((), (), s32[]{:S(2)}) async-start(), calls=%async_computation.15 | async-start | bytes 2162688 | tf_op jit(solution)/shard_map/reduce_scatter | solution.py:317
  908.0 24.3 collective-permute-start.3
  935.9 360.1 %reduce-scatter.12.cloned.1.call-start = ((), (), s32[]{:S(2)}) async-start(), calls=%async_computation.14 | async-start | bytes 2162688 | tf_op jit(solution)/shard_map/reduce_scatter | solution.py:316
  974.8 15.0 copy-start.29
  974.8 15.0 copy-start.31
  974.9 14.7 collective-permute-start.2
  990.8 2.3 copy-start.11
  993.1 442.8 %reduce-scatter.16.cloned.1.call-start = ((), (), s32[]{:S(2)}) async-start(), calls=%async_computation.16 | async-start | bytes 4325376 | tf_op jit(solution)/shard_map/reduce_scatter | solution.py:318
  997.6 579.0 %reduce-scatter.10.cloned.1.call-start = ((), (), s32[]{:S(2)}) async-start(), calls=%async_computation.13 | async-start | bytes 4325376 | tf_op jit(solution)/shard_map/reduce_scatter | solution.py:315
  1012.4 926.4 %reduce-scatter.20.cloned.1.call-start = ((), (), s32[]{:S(2)}) async-start(), calls=%async_computation.18 | async-start | bytes 34603008 | tf_op jit(solution)/shard_map/reduce_scatter | solution.py:223
  1037.7 1610.0 %reduce-scatter.18.cloned.1.call-start = ((), (), s32[]{:S(2)}) async-start(), calls=%async_computation.17 | async-start | bytes 69206016 | tf_op jit(solution)/shard_map/reduce_scatter | solution.py:222
  1078.0 2.3 copy-start.18
  1078.0 2.3 copy-start.24
  1078.0 2.5 copy-start.32
  1080.5 2.6 copy-start.60
  1080.5 44.3 %copy-start.56 = (f32[512]{0:T(512)S(1)}, f32[512]{0:T(512)}, u32[]{:S(2)}) copy-start(f32[512]{0:T(512)} %copy-done.55) | copy-start | bytes 6148
  (16 other events, 16.8 us)
Sparse Core Ops, SparseCore 0:
  9.6 23.7 all-gather.8
  34.9 21.3 all-gather.10
  57.8 33.1 all-gather.12
  92.3 33.1 all-gather.14
  126.9 391.1 all-gather.16
  519.5 201.0 all-gather.18
  894.6 129.0 reduce-scatter.21
  1026.6 133.2 reduce-scatter.13
  1162.7 133.2 reduce-scatter.11
  1298.8 137.0 reduce-scatter.15
  1438.8 137.7 reduce-scatter.9
  1579.4 359.2 reduce-scatter.19
  1941.8 705.8 reduce-scatter.17
where the time goes:
time: 2660 us; the launch traced here: 2650 us
  waiting for transfers between devices  1930 us (73%)
  matrix products  296 us (11%)
  local copies, waits for them, and re-layouts  271 us (10%)
  other arithmetic  79.3 us (3%)
  blocking collectives  51.4 us (2%)
    reduce_scatter x1, waiting for transfers between devices, on_device(): lax.psum_scatter(grad_in_weight, ('group', 'replica'), scatter_dimension=...  709 us
    reduce_scatter x1, waiting for transfers between devices, on_device(): lax.psum_scatter(grad_out_weight, ('group', 'replica'), scatter_dimension...  362 us
    all_gather x1, waiting for transfers between devices, on_device(): lax.all_gather(expert_in, 'group', axis=0, tiled=True)  218 us
    all_gather x1, waiting for transfers between devices, on_device(): lax.all_gather(expert_out, 'group', axis=0, tiled=True)  172 us
    reduce_scatter x1, waiting for transfers between devices, on_device(): lax.psum_scatter(query_full_grad, ('group', 'replica'), scatter_dimension...  141 us
    reduce_scatter x1, waiting for transfers between devices, on_device(): lax.psum_scatter(out_full_grad, ('group', 'replica'), scatter_dimension=1...  140 us
    reduce_scatter x1, waiting for transfers between devices, on_device(): lax.psum_scatter(key_full_grad, ('group', 'replica'), scatter_dimension=0...  136 us
  transfers between devices with their start and end apart: 17, of which 10 were waited for; matrix products, arithmetic and copies ran while one was open for 18% of the time, Pallas kernels for 0%

commit v1 on v0

--- a/solution.py
+++ b/solution.py
@@ -15,6 +15,27 @@
 THETA_BASE = 10000.0
 MASKED = -1e30
 HIGHEST = lax.Precision.HIGHEST
+
+
+def joined_along(parts, dim):
+    parts = jnp.moveaxis(parts, 0, dim)
+    shape = parts.shape
+    return parts.reshape(*shape[:dim], shape[dim] * shape[dim + 1], *shape[dim + 2 :])
+
+
+def grow_blocks(x, axis):
+    size, position = (lax.axis_size(axis), lax.axis_index(axis))
+    blocks, bit = (x[None], 1)
+    while bit < size:
+        theirs = lax.ppermute(blocks, axis, [(i, i ^ bit) for i in range(size)])
+        low = position & bit == 0
+        blocks = jnp.concatenate([jnp.where(low, blocks, theirs), jnp.where(low, theirs, blocks)])
+        bit *= 2
+    return blocks
+
+
+def gather_by_bits(shard, axis, dim):
+    return joined_along(grow_blocks(shard, axis), dim)
 
 
 def from_behind(value, axis, steps):
@@ -186,7 +207,7 @@
     gain_ffn, router_full, expert_in_full, expert_out_full = (
         lax.all_gather(ffn_gain, "group", axis=0, tiled=True),
         lax.all_gather(router_weight, "group", axis=0, tiled=True),
-        lax.all_gather(expert_in, "group", axis=0, tiled=True),
+        gather_by_bits(expert_in, "group", 0),
         lax.all_gather(expert_out, "group", axis=0, tiled=True),
     )
     normed_ffn_f, ffn_norm_pull = jax.vjp(normalize, residual, gain_ffn.astype(jnp.float32))

time: 2660 us -> 3010 us (1.13)
  blocking collectives: 51.4 us -> 675 us
  waiting for transfers between devices: 1930 us -> 1620 us
  other arithmetic: 79.3 us -> 124 us
    all_gather x1, blocking collectives: 3.74 us -> 624 us  [on_device(): lax.all_gather(attn_gain, 'group', axis=0, tiled=True)]
    all_gather x1, waiting for transfers between devices: 218 us -> 0.02 us  [on_device(): lax.all_gather(expert_in, 'group', axis=0, tiled=True)]
    all_gather x1, waiting for transfers between devices: 172 us -> 0.01 us  [on_device(): lax.all_gather(expert_out, 'group', axis=0, tiled=True)]
    reduce_scatter x1, waiting for transfers between devices: 31.6 us -> 136 us  [on_device(): lax.psum_scatter(value_full_grad, ('group', 'replica'), scatter_dimension...]
    reduce_scatter x1, waiting for transfers between devices: 136 us -> 80.4 us  [on_device(): lax.psum_scatter(key_full_grad, ('group', 'replica'), scatter_dimension=0...]
  transfers between devices with their start and end apart: 17 -> 18, of which waited for: 10 -> 10; matrix products, arithmetic and copies ran while one was open for 18% -> 18% of each run, Pallas kernels for 0% -> 0%
where the time goes in v1:
time: 3010 us; the launch traced here: 3000 us
  waiting for transfers between devices  1620 us (54%)
  blocking collectives  675 us (22%)
  matrix products  282 us (9%)
  local copies, waits for them, and re-layouts  273 us (9%)
  other arithmetic  124 us (4%)
    reduce_scatter x1, waiting for transfers between devices, on_device(): lax.psum_scatter(grad_in_weight, ('group', 'replica'), scatter_dimension=...  709 us
    all_gather x1, blocking collectives, on_device(): lax.all_gather(attn_gain, 'group', axis=0, tiled=True)  624 us
    reduce_scatter x1, waiting for transfers between devices, on_device(): lax.psum_scatter(grad_out_weight, ('group', 'replica'), scatter_dimension...  363 us
    reduce_scatter x1, waiting for transfers between devices, on_device(): lax.psum_scatter(query_full_grad, ('group', 'replica'), scatter_dimension...  140 us
    reduce_scatter x1, waiting for transfers between devices, on_device(): lax.psum_scatter(out_full_grad, ('group', 'replica'), scatter_dimension=1...  140 us
    reduce_scatter x1, waiting for transfers between devices, on_device(): lax.psum_scatter(value_full_grad, ('group', 'replica'), scatter_dimension...  136 us
    reduce_scatter x1, waiting for transfers between devices, on_device(): lax.psum_scatter(key_full_grad, ('group', 'replica'), scatter_dimension=0...  80.4 us
  transfers between devices with their start and end apart: 18, of which 10 were waited for; matrix products, arithmetic and copies ran while one was open for 18% of the time, Pallas kernels for 0%

profile of v1, /device:TPU:1, one launch (start us, length us, event | category | flops | bytes accessed | tf_op | source)
XLA Modules:
  0.0 2996.9 jit_solution(10986001346835998087)
XLA Ops:
  11.2 2.1 collective-permute-start.2
  13.3 624.3 %all-gather = bf16[2,1,512]{2,1,0:T(2,128)(2,1)S(1)} all-gather(bf16[1,1,512]{2,1,0:T(2,128)(2,1)S(1)} %reshape.599), channel_id=1, replica_groups=mesh['group'=2,'replica'=16] {'group'}, dimensions={0}, use_global_device_ids=true | all-gather | bytes 3072 | tf_op jit(solution)/shard_map/all_gather | solution.py:155
  638.4 4.3 all-gather.1
  647.5 15.5 scatter_custom_fusion
  663.0 28.6 scatter_custom_fusion.1
  692.5 27.2 gather_fusion.2
  719.8 24.8 copy.88
  744.6 4.0 all_gather.34
  749.9 1.6 or_and_fusion
  751.5 1.5 copy.75
  755.0 4.2 collective-permute-start.1
  759.2 2.1 convolution_convert_fusion.1
  761.3 1.5 collective-permute-start
  762.9 3.9 copy.76
  766.8 3.0 fusion.45
  770.2 9.5 collective-permute-done.1
  779.7 14.5 fusion.91
  794.2 13.1 fusion.3
  807.4 13.9 fusion.41
  821.4 3.3 multiply_reduce_fusion.2
  826.3 26.9 gather_fusion
  853.6 33.0 %gather_fusion.4 = f32[4096]{0:T(1024)S(1)} fusion(f32[512,16]{0,1:T(8,128)S(1)} %fusion.92, s32[4096]{0:T(1024)S(1)} %copy-done.4), kind=kCustom, calls=%fused_computation.4 | custom fusion | bytes 65536 | tf_op jit(solution)/shard_map/jit(take_along_axis)/gather | solution.py:216
  887.8 15.7 scatter_custom_fusion.2
  903.5 17.1 copy.85
  922.2 22.6 broadcast_select_fusion.1
  944.8 22.7 pad_maximum_fusion
  967.5 28.1 fusion.14
  995.7 30.3 %multiply_convert_fusion.2 = (bf16[16,384,512]{2,1,0:T(8,128)(2,1)}, bf16[16,384,512]{2,1,0:T(8,128)(2,1)}, bf16[16,384,512]{2,1,0:T(8,128)(2,1)}) fusion(f32[16,384,1024]{2,1,0:T(8,128)} %fusion.14, bf16[16,1024,512]{2,1,0:T(8,128)(2,1)} %all-gather.17.cloned.1.call-done, f32[16,384,1024]{1,2,0:T(8,128)} %copy.88, f32[16,384]{1,0:T(8,128)S(1)} %mul.437), kind=kOutput, calls=%fused_computation.33 | convolution fusion | flops 6502219776 | bytes 86007808 | tf_op jit(solution)/shard_map/ecd,edf->ecf/dot_general | solution.py:104
  1026.0 18.3 fusion.93
  1044.3 30.6 %gather_fusion.1 = f32[4096,1024]{1,0:T(8,128)} fusion(f32[6144,1024]{1,0:T(8,128)} %bitcast.198, s32[4096]{0:T(1024)S(1)} %copy-done.51), kind=kCustom, calls=%fused_computation.1 | custom fusion | bytes 33570816 | tf_op jit(solution)/shard_map/gather | solution.py:229
  1075.0 10.8 fusion.8
  1086.2 26.4 fusion.16
  1112.6 30.5 %gather_fusion.3 = f32[4096,1024]{1,0:T(8,128)} fusion(f32[6144,1024]{1,0:T(8,128)} %bitcast.199, s32[4096]{0:T(1024)S(1)} %copy-done.51), kind=kCustom, calls=%fused_computation.3 | custom fusion | bytes 33570816 | tf_op jit(solution)/shard_map/gather | solution.py:247
  1143.1 8.2 bitcast_reduce_fusion
  1151.4 2.2 multiply_reduce_fusion
  1153.6 1.6 fusion.34
  1158.4 21.7 fusion
  1180.1 27.8 fusion.2
  1208.0 12.3 fusion.37
  1220.3 2.2 slice.125
  1223.8 2.0 fusion.96
  1225.9 7.0 collective-permute-done.3
  1232.9 1.5 slice_add_fusion.1
  1235.5 2.3 fusion.53
  1237.8 14.7 fusion.38
  1253.8 1.4 collective-permute-start.4
  1255.2 9.0 collective-permute-done.4
  1265.7 2.3 fusion.51
  1268.3 8.9 convolution_multiply_fusion
  1278.6 3.4 fusion.49
  1283.3 4.9 fusion.58
  1288.9 24.6 fusion.19
  1314.2 33.6 %fusion.12 = f32[16,1024,1024]{2,1,0:T(8,128)} fusion(bf16[16,384,1024]{1,2,0:T(8,128)(2,1)} %copy.85, bf16[16,384,512]{2,1,0:T(8,128)(2,1)} %get-tuple-element.71, bf16[16,384,512]{2,1,0:T(8,128)(2,1)} %get-tuple-element.70, bf16[16,384]{1,0:T(8,128)(2,1)S(1)} %copy-done.46), kind=kOutput, calls=%fused_computation.37 | convolution fusion | flops 12916359168 | bytes 92286976 | tf_op jit(solution)/shard_map/ecd,ecf->edf/dot_general | solution.py:116
  1347.9 18.0 reduce-scatter.22.cloned.1.call-done
  1367.3 3.0 fusion.94
  1371.5 2.5 fusion.29
  1374.0 42.5 %all-reduce.2 = (f32[1024]{0:T(1024)S(1)}, f32[1024]{0:T(1024)S(1)}) all-reduce(f32[1024]{0:T(1024)S(1)} %get-tuple-element.66, f32[1024]{0:T(1024)S(1)} %copy-done.67), channel_id=2, replica_groups=mesh['group'=2,'replica'=16] {'group','replica'}, use_global_device_ids=true, to_apply=%region_22.23.clone | all-reduce | flops 2048 | bytes 16384
  1417.7 4.1 fusion.36
  1421.8 80.4 %reduce-scatter.12.cloned.1.call-done = f32[32,512]{1,0:T(8,128)} async-done(((f32[1024,512]{1,0:T(8,128)}), f32[32,512]{1,0:T(8,128)}) %reduce-scatter.12.cloned.1.call-update) | async-done | bytes 65552 | tf_op jit(solution)/shard_map/reduce_scatter | solution.py:337
  1502.1 135.8 %reduce-scatter.14.cloned.1.call-done = f32[32,512]{1,0:T(8,128)} async-done(((f32[1024,512]{1,0:T(8,128)}), f32[32,512]{1,0:T(8,128)}) %reduce-scatter.14.cloned.1.call-update) | async-done | bytes 65552 | tf_op jit(solution)/shard_map/reduce_scatter | solution.py:338
  1638.0 140.3 %reduce-scatter.10.cloned.1.call-done = f32[32,1024]{1,0:T(8,128)} async-done(((f32[1024,1024]{1,0:T(8,128)}), f32[32,1024]{1,0:T(8,128)}) %reduce-scatter.10.cloned.1.call-update) | async-done | bytes 131088 | tf_op jit(solution)/shard_map/reduce_scatter | solution.py:336
  1778.3 139.9 %reduce-scatter.16.cloned.1.call-done = f32[1024,32]{0,1:T(8,128)} async-done(((f32[1024,1024]{0,1:T(8,128)}), f32[1024,32]{0,1:T(8,128)}) %reduce-scatter.16.cloned.1.call-update) | async-done | bytes 131088 | tf_op jit(solution)/shard_map/reduce_scatter | solution.py:339
  1918.1 362.7 %reduce-scatter.20.cloned.1.call-done = f32[16,32,512]{2,1,0:T(8,128)} async-done(((f32[16,1024,512]{2,1,0:T(8,128)}), f32[16,32,512]{2,1,0:T(8,128)}) %reduce-scatter.20.cloned.1.call-update) | async-done | bytes 1048592 | tf_op jit(solution)/shard_map/reduce_scatter | solution.py:244
  2280.9 709.0 %reduce-scatter.18.cloned.1.call-done = f32[16,32,1024]{2,1,0:T(8,128)} async-done(((f32[16,1024,1024]{2,1,0:T(8,128)}), f32[16,32,1024]{2,1,0:T(8,128)}) %reduce-scatter.18.cloned.1.call-update) | async-done | bytes 2097168 | tf_op jit(solution)/shard_map/reduce_scatter | solution.py:243
  (249 shorter events, 34.7 us)
Async XLA Ops:
  7.2 744.3 %all-gather.11.cloned.1.call-start = ((), (), s32[]{:S(2)}) async-start(), calls=%async_computation.8 | async-start | bytes 1572864 | tf_op jit(solution)/shard_map/all_gather | solution.py:157
  7.9 751.3 %all-gather.9.cloned.1.call-start = ((), (), s32[]{:S(2)}) async-start(), calls=%async_computation.7 | async-start | bytes 1572864 | tf_op jit(solution)/shard_map/all_gather | solution.py:158
  8.7 754.2 %all-gather.13.cloned.1.call-start = ((), (), s32[]{:S(2)}) async-start(), calls=%async_computation.9 | async-start | bytes 3145728 | tf_op jit(solution)/shard_map/all_gather | solution.py:156
  9.4 812.0 %all-gather.15.cloned.1.call-start = ((), (), s32[]{:S(2)}) async-start(), calls=%async_computation.10 | async-start | bytes 3145728 | tf_op jit(solution)/shard_map/all_gather | solution.py:159
  10.0 985.7 %all-gather.17.cloned.1.call-start = ((), (), s32[]{:S(2)}) async-start(), calls=%async_computation.11 | async-start | bytes 25165824 | tf_op jit(solution)/shard_map/all_gather | solution.py:211
  10.6 627.8 %copy-start.69 = (bf16[512]{0:T(512)(128)(2,1)S(1)}, bf16[512]{0:T(512)(128)(2,1)}, u32[]{:S(2)}) copy-start(bf16[512]{0:T(512)(128)(2,1)} %param.19) | copy-start | bytes 3076
  10.6 632.7 %copy-start.38 = (s32[1,512,8]{1,2,0:T(8,128)S(1)}, s32[1,512,8]{1,2,0:T(8,128)}, u32[]{:S(2)}) copy-start(s32[1,512,8]{1,2,0:T(8,128)} %param.23) | copy-start | bytes 49156
  10.6 681.7 %copy-start.18 = (bf16[1,512,1024]{2,1,0:T(8,128)(2,1)S(1)}, bf16[1,512,1024]{2,1,0:T(8,128)(2,1)}, u32[]{:S(2)}) copy-start(bf16[1,512,1024]{2,1,0:T(8,128)(2,1)} %param.25) | copy-start | bytes 3145732
  10.6 1075.6 %all-gather.19.cloned.1.call-start = ((), (), s32[]{:S(2)}) async-start(), calls=%async_computation.12 | async-start | bytes 50331648 | tf_op jit(solution)/shard_map/all_gather | solution.py:236
  11.2 1354.7 %reduce-scatter.22.cloned.1.call-start = ((), (), s32[]{:S(2)}) async-start(), calls=%async_computation.19 | async-start | bytes 540672
  11.2 911.0 %collective-permute-start.2 = (bf16[1,8,1024,1024]{3,2,1,0:T(8,128)(2,1)}, bf16[1,8,1024,1024]{3,2,1,0:T(8,128)(2,1)}, u32[]{:S(2)}, u32[]{:S(2)}) collective-permute-start(bf16[1,8,1024,1024]{3,2,1,0:T(8,128)(2,1)} %bitcast.201), channel_id=1, source_target_pairs={{0,16},{16,0},{1,17},{17,1},{2,18},{18,2},{3,19},{19,3},{4,20},{20... | collective-permute-start | bytes 50331656 | tf_op jit(solution)/shard_map/ppermute | solution.py:30
  637.7 129.1 %copy-start.52 = (f32[2,1,512]{2,1,0:T(1,128)}, f32[2,1,512]{2,1,0:T(1,128)S(1)}, u32[]{:S(2)}) copy-start(f32[2,1,512]{2,1,0:T(1,128)S(1)} %convert_element_type.171) | copy-start | bytes 12292
  643.4 48.9 %copy-start.13 = (s32[1,512,8]{2,1,0:T(8,128)}, s32[1,512,8]{2,1,0:T(8,128)S(1)}, u32[]{:S(2)}) copy-start(s32[1,512,8]{2,1,0:T(8,128)S(1)} %copy.78) | copy-start | bytes 49156
  647.5 101.5 %copy-start.55 = (s32[4096,1]{0,1:T(1,128)}, s32[4096,1]{0,1:T(1,128)S(1)}, u32[]{:S(2)}) copy-start(s32[4096,1]{0,1:T(1,128)S(1)} %compare_select_fusion.1) | copy-start | bytes 49156
  692.5 27.3 copy-start
  719.8 24.8 copy-start.66
  719.8 28.9 copy-start.5
  748.6 104.6 %copy-start.47 = (bf16[1024,16]{0,1:T(8,128)(2,1)}, bf16[1024,16]{0,1:T(8,128)(2,1)S(1)}, u32[]{:S(2)}) copy-start(bf16[1024,16]{0,1:T(8,128)(2,1)S(1)} %all_gather.34) | copy-start | bytes 98308
  749.0 17.8 copy-start.58
  749.9 19.9 copy-start.30
  749.9 19.9 copy-start.32
  754.0 25.7 copy-start.21
  754.0 25.7 copy-start.23
  755.0 24.7 collective-permute-start.1
  761.3 46.1 %copy-start.40 = (bf16[512,512]{0,1:T(8,128)(2,1)}, bf16[512,512]{0,1:T(8,128)(2,1)S(1)}, u32[]{:S(2)}) copy-start(bf16[512,512]{0,1:T(8,128)(2,1)S(1)} %convolution_convert_fusion.1) | copy-start | bytes 1572868
  761.3 46.1 %collective-permute-start = (bf16[512,8,64]{0,2,1:T(8,128)(2,1)S(1)}, bf16[512,8,64]{0,2,1:T(8,128)(2,1)S(1)}, u32[]{:S(2)}, u32[]{:S(2)}) collective-permute-start(bf16[512,8,64]{0,2,1:T(8,128)(2,1)S(1)} %bitcast.229), channel_id=1, source_target_pairs={{0,16},{1,17},{2,18},{3,19},{4,20},{5,21},{6,22},{7,23},{8,24},{9,... | collective-permute-start | bytes 1572872 | tf_op jit(solution)/shard_map/ppermute | solution.py:44
  766.8 12.9 copy-start.44
  770.2 24.0 copy-start.25
  770.2 24.0 copy-start.27
  807.4 14.0 copy-start.42
  824.7 28.4 copy-start.64
  824.7 28.4 copy-start.60
  826.3 26.9 copy-start.2
  826.3 27.3 copy-start.4
  853.6 33.2 %copy-start.14 = (s32[1,512,8]{2,1,0:T(8,128)S(1)}, s32[1,512,8]{2,1,0:T(8,128)}, u32[]{:S(2)}) copy-start(s32[1,512,8]{2,1,0:T(8,128)} %copy-done.13) | copy-start | bytes 49156
  853.6 34.2 %copy-start.54 = (s32[4096]{0:T(1024)S(1)}, s32[4096]{0:T(1024)}, u32[]{:S(2)}) copy-start(s32[4096]{0:T(1024)} %squeeze.32) | copy-start | bytes 49156
  903.5 92.1 %copy-start.49 = (f32[16,384]{1,0:T(8,128)}, f32[16,384]{1,0:T(8,128)S(1)}, u32[]{:S(2)}) copy-start(f32[16,384]{1,0:T(8,128)S(1)} %mul.437) | copy-start | bytes 73732
  944.8 22.7 copy-start.45
  1026.0 18.3 copy-start.51
  1044.3 30.6 %copy-start.1 = (f32[512,1024]{1,0:T(8,128)S(1)}, f32[512,1024]{1,0:T(8,128)}, u32[]{:S(2)}) copy-start(f32[512,1024]{1,0:T(8,128)} %copy-done) | copy-start | bytes 6291460
  1044.3 30.6 %copy-start.17 = (f32[512,8]{1,0:T(8,128)S(1)}, f32[512,8]{1,0:T(8,128)}, u32[]{:S(2)}) copy-start(f32[512,8]{1,0:T(8,128)} %fusion.61) | copy-start | bytes 49156
  1075.0 11.2 copy-start.39
  1143.1 8.2 copy-start.57
  1143.1 8.2 copy-start.61
  1180.1 27.9 copy-start.26
  1180.1 27.9 copy-start.28
  1208.0 15.8 copy-start.3
  1220.3 14.1 copy-start.31
  1220.3 14.1 copy-start.33
  1220.3 15.1 copy-start.6
  1220.3 15.2 copy-start.53
  1220.3 15.1 copy-start.59
  1222.5 10.3 collective-permute-start.3
  1225.9 276.3 %reduce-scatter.12.cloned.1.call-start = ((), (), s32[]{:S(2)}) async-start(), calls=%async_computation.14 | async-start | bytes 2162688 | tf_op jit(solution)/shard_map/reduce_scatter | solution.py:337
  1237.8 400.2 %reduce-scatter.14.cloned.1.call-start = ((), (), s32[]{:S(2)}) async-start(), calls=%async_computation.15 | async-start | bytes 2162688 | tf_op jit(solution)/shard_map/reduce_scatter | solution.py:338
  1253.8 14.5 copy-start.22
  1253.8 14.5 copy-start.24
  1253.8 10.5 collective-permute-start.4
  1267.9 510.3 %reduce-scatter.10.cloned.1.call-start = ((), (), s32[]{:S(2)}) async-start(), calls=%async_computation.13 | async-start | bytes 4325376 | tf_op jit(solution)/shard_map/reduce_scatter | solution.py:336
  1282.1 636.1 %reduce-scatter.16.cloned.1.call-start = ((), (), s32[]{:S(2)}) async-start(), calls=%async_computation.16 | async-start | bytes 4325376 | tf_op jit(solution)/shard_map/reduce_scatter | solution.py:339
  1288.2 992.7 %reduce-scatter.20.cloned.1.call-start = ((), (), s32[]{:S(2)}) async-start(), calls=%async_computation.18 | async-start | bytes 34603008 | tf_op jit(solution)/shard_map/reduce_scatter | solution.py:244
  1313.6 1676.3 %reduce-scatter.18.cloned.1.call-start = ((), (), s32[]{:S(2)}) async-start(), calls=%async_computation.17 | async-start | bytes 69206016 | tf_op jit(solution)/shard_map/reduce_scatter | solution.py:243
  1347.9 19.4 copy-start.36
  1371.5 46.1 %copy-start.63 = (f32[512]{0:T(512)S(1)}, f32[512]{0:T(512)}, u32[]{:S(2)}) copy-start(f32[512]{0:T(512)} %copy-done.62) | copy-start | bytes 6148
  (24 other events, 64.3 us)
Sparse Core Ops, SparseCore 0:
  9.6 34.9 all-gather.10
  46.1 32.6 all-gather.8
  80.3 55.6 all-gather.12
  137.5 55.6 all-gather.14
  194.6 378.7 all-gather.16
  574.8 428.4 all-gather.18
  1226.0 139.8 reduce-scatter.21
  1368.8 133.2 reduce-scatter.11
  1505.0 132.9 reduce-scatter.13
  1640.8 137.4 reduce-scatter.9
  1781.2 136.8 reduce-scatter.15
  1921.0 359.8 reduce-scatter.19
  2283.9 705.8 reduce-scatter.17
